TPU v7x, 768 devices: a whole 4x8x12 slice. The times are simulated.
768 devices in a mesh: dp: 24 (over z_hi, y), frame: 8 (over z_lo, core), mp: 4 (over x).
Axes of the slice: x: 4, y: 8, z: 12 (z_hi: 3, z_lo: 4; z = z_hi * 4 + z_lo), core: 2. Of those that a mesh axis runs over, the one named last changes fastest.
Arguments:
- projected: bfloat16 [6, 24, 16, 128, 5120], P(None, 'dp', 'frame', None, 'mp'), may hold values from -6 to 6
- codes: float32 [24, 16, 32], P('dp'), may hold values from -6 to 6
- action_weight: float32 [32, 5120], P(None, 'mp'), may hold values from -1 to 1
- clip_ids: int32 [24], replicated, may hold values from 0 to 23, each once
- frame_map: int32 [16], replicated, may hold values from 0 to 15, each once
- segments: int32 [24, 16], P('dp'), may hold values from 0 to 2, never falling along the last dimension, each value on 1 to 8 neighbouring positions
Outputs:
- mixed: bfloat16 [24, 16, 128, 5120], P('dp', 'frame', None, 'mp')
Inputs may be any that keep to these rules, and one draw needn't show every extreme that they name: `clip_ids`: each clip id appears once. `frame_map`: each time appears once. `segments`: episode numbers never fall along time.
All inputs are finite; a program needn't handle non-finite values.
Results may differ from a plain program's by a relative error of at most 0.0085.
Values may be sent and summed in bfloat16 or wider, within the bound.
A program may use at most 32 MiB of HBM per device.

v0:
```python
import jax
import jax.numpy as jnp
from jax import lax
from jax.sharding import PartitionSpec as P

E = 128


def masked_softmax(spatial_scores, allowed):
    peak = jnp.max(jnp.where(allowed, spatial_scores, -1e30), axis=-1, keepdims=True)
    weights = jnp.where(allowed, jnp.exp(spatial_scores - peak), 0.0)
    return (weights / jnp.sum(weights, axis=-1, keepdims=True)).astype(jnp.bfloat16)


def local(projected, codes, action_weight, clip_ids, frame_map, segments):
    clip_dev, frames_dev, patches, width = projected.shape[1:]
    heads_dev = width // E
    frames_all = frame_map.shape[0]
    score_scale = 1.0 / E**0.5
    head_patches = lax.Precision.HIGHEST
    reshaped_rows = projected.reshape(6, clip_dev, frames_dev, patches, heads_dev, E)
    all_codes = lax.all_gather(codes, "dp", axis=0, tiled=True)
    owned = lax.axis_index("dp") * clip_dev + jnp.arange(clip_dev, dtype=jnp.int32)
    select = (clip_ids[:, None] == owned[None, :]).astype(jnp.float32)
    by_clip = jnp.einsum("ic,ifa->cfa", select, all_codes, precision=head_patches)
    local_times = lax.dynamic_slice_in_dim(
        frame_map, lax.axis_index("frame") * frames_dev, frames_dev
    )
    pick = (local_times[:, None] == jnp.arange(frames_all, dtype=jnp.int32)[None, :]).astype(
        jnp.float32
    )
    codes_slot = jnp.einsum("st,cta->csa", pick, by_clip, precision=head_patches)
    action_rows = jnp.einsum("csa,ad->csd", codes_slot, action_weight, precision=head_patches)
    values_t = (
        reshaped_rows[5].astype(jnp.float32)
        + action_rows.reshape(clip_dev, frames_dev, 1, heads_dev, E)
    ).astype(jnp.bfloat16)
    temporal_in = jnp.stack([reshaped_rows[3], reshaped_rows[4], values_t])
    match = frame_map[:, None] == jnp.arange(frames_all, dtype=jnp.int32)[None, :]
    seg_slot = jnp.sum(jnp.where(match[None], segments[:, None, :], 0), axis=-1)
    allowed = (frame_map[None, :] <= frame_map[:, None])[None] & (
        seg_slot[:, None, :] == seg_slot[:, :, None]
    )
    gathered = lax.all_to_all(temporal_in, "frame", split_axis=3, concat_axis=2, tiled=True)
    tscores = (
        jnp.einsum(
            "csphe,ctphe->cphst", gathered[0], gathered[1], preferred_element_type=jnp.float32
        )
        * score_scale
    )
    tprobs = masked_softmax(tscores, allowed[:, None, None])
    finished = jnp.einsum(
        "cphst,ctphe->csphe", tprobs, gathered[2], preferred_element_type=jnp.float32
    ).astype(jnp.bfloat16)
    temporal = lax.all_to_all(finished, "frame", split_axis=1, concat_axis=2, tiled=True)
    spatial_scores = (
        jnp.einsum(
            "cfphe,cfqhe->cfhpq",
            reshaped_rows[0],
            reshaped_rows[1],
            preferred_element_type=jnp.float32,
        )
        * score_scale
    )
    probs = masked_softmax(spatial_scores, jnp.ones((1, 1, 1, 1, 1), bool))
    spatial = jnp.einsum(
        "cfhpq,cfqhe->cfphe", probs, reshaped_rows[2], preferred_element_type=jnp.float32
    ).astype(jnp.bfloat16)
    mixed = (spatial.astype(jnp.float32) + temporal.astype(jnp.float32)).astype(jnp.bfloat16)
    return mixed.reshape(clip_dev, frames_dev, patches, width)


def solution(mesh):
    return jax.shard_map(
        local,
        mesh=mesh,
        in_specs=(
            P(None, "dp", "frame", None, "mp"),
            P("dp", None, None),
            P(None, "mp"),
            P(),
            P(),
            P("dp", None),
        ),
        out_specs=P("dp", "frame", None, "mp"),
        check_vma=False,
    )
```

profile of v0, /device:TPU:1, one launch (start us, length us, event | category | flops | bytes accessed | tf_op | source)
XLA Modules:
  0.0 183.6 jit_solution(1229005692687429717)
XLA Ops:
  0.0 74.7 %all_gather.3 = f32[24,16,32]{2,1,0:T(8,128)S(1)} all-gather(f32[1,16,32]{2,1,0:T(8,128)} %param.7), channel_id=1, replica_groups=mesh['dp'=24,'frame'=8,'mp'=4] {'dp'}, dimensions={0}, use_global_device_ids=true | all-gather | bytes 51200 | tf_op jit(solution)/shard_map/all_gather | solution.py:22
  74.7 0.7 dynamic_slice.3
  75.4 0.9 fusion.22
  76.7 3.4 %fusion.36 = (bf16[1,1,2,128,1280]{4,3,2,1,0:T(8,128)(2,1)S(1)}, bf16[1,1,2,128,1280]{4,3,2,1,0:T(8,128)(2,1)S(1)}, bf16[1,1,2,128,1280]{4,3,2,1,0:T(8,128)(2,1)...) fusion(bf16[6,1,2,128,1280]{4,3,2,1,0:T(8,128)(2,1)} %param.6), kind=kLoop, calls=%fused_computation.46 | loop fusion | bytes 7864320 | tf_op jit(solution)/shard_map/slice | solution.py:60
  80.1 1.4 copy.129
  81.5 1.1 copy.127
  82.6 1.1 copy.128
  83.7 0.4 fusion.16
  84.1 0.7 copy-done.2
  85.2 4.7 %copy.108 = bf16[3,1,2,128,10,128]{5,2,4,1,0,3:T(2,128)(2,1)} copy(bf16[3,1,2,128,10,128]{3,5,4,2,1,0:T(8,128)(2,1)S(1)} %pad_maximum_fusion) | data formatting | bytes 3932160 | tf_op jit(solution)/shard_map/stack | solution.py:38
  89.9 16.4 %all-to-all-start = ((bf16[3,1,2,128,10,128]{5,2,4,1,0,3:T(2,128)(2,1)}), bf16[3,1,2,128,10,128]{5,2,4,1,0,3:T(2,128)(2,1)S(1)}, u32[]{:S(2)}, u32[]{:S(2)}) async-start(bf16[3,1,2,128,10,128]{5,2,4,1,0,3:T(2,128)(2,1)} %copy.108), calls=%async_computation | async-start | bytes 3932160 | tf_op jit(solution)/shard_map/all_to_all | solution.py:44
  106.6 45.0 %all-to-all-done = bf16[3,1,2,128,10,128]{5,2,4,1,0,3:T(2,128)(2,1)S(1)} async-done(((bf16[3,1,2,128,10,128]{5,2,4,1,0,3:T(2,128)(2,1)}), bf16[3,1,2,128,10,128]{5,2,4,1,0,3:T(2,128)(2,1)S(1)}, u32[]{:S(2)}, u32[]{:S(2)}) %all-to-all-start) | async-done | bytes 1966112 | tf_op jit(solution)/shard_map/all_to_all | solution.py:44
  151.6 0.5 copy.109
  152.1 0.5 fusion.37
  152.6 0.7 copy.111
  153.2 0.7 copy.112
  153.9 0.7 copy.110
  154.6 0.5 convolution_multiply_fusion
  155.1 0.6 fusion.38
  155.7 0.4 fusion.17
  156.1 1.1 copy.114
  157.2 4.4 %all-to-all-start.1 = ((bf16[1,16,16,10,128]{4,2,3,0,1:T(8,128)(2,1)}), bf16[1,16,16,10,128]{4,2,3,0,1:T(8,128)(2,1)S(1)}, u32[]{:S(2)}, u32[]{:S(2)}) async-start(bf16[1,16,16,10,128]{4,2,3,0,1:T(8,128)(2,1)} %copy.114), calls=%async_computation.1 | async-start | bytes 1310720 | tf_op jit(solution)/shard_map/all_to_all | solution.py:55
  161.7 0.3 copy.125
  162.0 0.3 copy.126
  162.3 1.1 copy.101
  163.4 0.6 fusion.39
  164.0 1.5 convolution_multiply_fusion.1
  165.5 13.4 %all-to-all-done.1 = bf16[1,16,16,10,128]{4,2,3,0,1:T(8,128)(2,1)S(1)} async-done(((bf16[1,16,16,10,128]{4,2,3,0,1:T(8,128)(2,1)}), bf16[1,16,16,10,128]{4,2,3,0,1:T(8,128)(2,1)S(1)}, u32[]{:S(2)}, u32[]{:S(2)}) %all-to-all-start.1) | async-done | bytes 655392 | tf_op jit(solution)/shard_map/all_to_all | solution.py:55
  179.2 0.4 copy.117
  179.6 0.7 copy-done.4
  180.2 2.3 %fusion.15 = bf16[1,2,128,10,128]{2,4,3,1,0:T(8,128)(2,1)S(1)} fusion(f32[1,2,128,10,128]{2,4,3,1,0:T(8,128)S(1)} %copy.117, bf16[2,128,10,128]{1,3,2,0:T(8,128)(2,1)S(1)} %bitcast.80, f32[2,10,128]{2,1,0:T(8,128)S(1)} %fusion.39, f32[2,10,128,128]{2,3,1,0:T(8,128)} %convolution_multiply_fusion.1), kind=kOutput, calls=%fused_computation.16 | convolution fusion | flops 86182528 | bytes 3942400 | tf_op jit(solution)/shard_map/cfhpq,cfqhe->cfphe/dot_general | solution.py:66
  182.5 1.1 copy.118
  (20 shorter events, 1.4 us)
Async XLA Ops:
  0.0 76.5 %copy-start = (f32[32,1280]{1,0:T(8,128)S(1)}, f32[32,1280]{1,0:T(8,128)}, u32[]{:S(2)}) copy-start(f32[32,1280]{1,0:T(8,128)} %param.8) | copy-start | bytes 491524
  83.7 1.1 copy-start.2
  83.7 1.3 copy-start.3
  89.9 16.4 %copy-start.5 = (s32[16]{0:T(128)S(1)}, s32[16]{0:T(128)}, u32[]{:S(2)}) copy-start(s32[16]{0:T(128)} %param.10) | copy-start | bytes 196
  89.9 16.4 %copy-start.6 = (s32[1,16]{1,0:T(1,128)S(1)}, s32[1,16]{1,0:T(1,128)}, u32[]{:S(2)}) copy-start(s32[1,16]{1,0:T(1,128)} %param.11) | copy-start | bytes 196
  89.9 61.7 %all-to-all-start = ((bf16[3,1,2,128,10,128]{5,2,4,1,0,3:T(2,128)(2,1)}), bf16[3,1,2,128,10,128]{5,2,4,1,0,3:T(2,128)(2,1)S(1)}, u32[]{:S(2)}, u32[]{:S(2)}) async-start(bf16[3,1,2,128,10,128]{5,2,4,1,0,3:T(2,128)(2,1)} %copy.108), calls=%async_computation | async-start | bytes 3932160 | tf_op jit(solution)/shard_map/all_to_all | solution.py:44
  156.1 5.5 %copy-start.1 = (bf16[1,1,2,128,1280]{4,3,2,1,0:T(8,128)(2,1)S(1)}, bf16[1,1,2,128,1280]{4,3,2,1,0:T(8,128)(2,1)}, u32[]{:S(2)}) copy-start(bf16[1,1,2,128,1280]{4,3,2,1,0:T(8,128)(2,1)} %get-tuple-element.8) | copy-start | bytes 1966084
  157.2 21.6 %all-to-all-start.1 = ((bf16[1,16,16,10,128]{4,2,3,0,1:T(8,128)(2,1)}), bf16[1,16,16,10,128]{4,2,3,0,1:T(8,128)(2,1)S(1)}, u32[]{:S(2)}, u32[]{:S(2)}) async-start(bf16[1,16,16,10,128]{4,2,3,0,1:T(8,128)(2,1)} %copy.114), calls=%async_computation.1 | async-start | bytes 1310720 | tf_op jit(solution)/shard_map/all_to_all | solution.py:55
  179.2 1.1 copy-start.4
where the time goes:
time: 184 us
  blocking collectives  74.7 us (41%)
  waiting for transfers between devices  58.4 us (32%)
  local copies, waits for them, and re-layouts  21.5 us (12%)
  starting transfers between devices  20.9 us (11%)
  matrix products  6.48 us (4%)
    all_gather x1, blocking collectives, local(): all_codes = lax.all_gather(codes, 'dp', axis=0, tiled=True)  74.7 us
    all_to_all x1, waiting for transfers between devices, local(): lax.all_to_all(temporal_in, 'frame', split_axis=3, concat_axis=2, tiled=T...  45 us
    all_to_all x1, starting transfers between devices, local(): lax.all_to_all(temporal_in, 'frame', split_axis=3, concat_axis=2, tiled=T...  16.4 us
    all_to_all x1, waiting for transfers between devices, local(): lax.all_to_all(finished, 'frame', split_axis=1, concat_axis=2, tiled=True)  13.4 us
    unnamed x19, local copies, waits for them, and re-layouts  5.8 us
    another operation x1, local copies, waits for them, and re-layouts, local(): temporal_in = jnp.stack([reshaped_rows[3], reshaped_rows[4], values_t])  4.72 us
    all_to_all x1, starting transfers between devices, local(): lax.all_to_all(finished, 'frame', split_axis=1, concat_axis=2, tiled=True)  4.41 us
  transfers between devices with their start and end apart: 2, of which 2 were waited for; matrix products, arithmetic and copies ran while one was open for 2% of the time, Pallas kernels for 0%

commit v1 on v0

v1 whole, which is shorter than its diff:
```python
import functools

import jax
import jax.numpy as jnp
from jax import lax
from jax.experimental import pallas as pl
from jax.experimental.pallas import tpu as pltpu
from jax.sharding import PartitionSpec as P

MESH = pl.DeviceIdType.MESH
E = 128
FAR = 3
HEADS = 2


def softmax(scores):
    peak = jnp.max(scores, axis=-1, keepdims=True)
    weights = jnp.exp(scores - peak)
    return (weights / jnp.sum(weights, axis=-1, keepdims=True)).astype(jnp.bfloat16)


def scores_of(q, k):
    return lax.dot_general(
        q, k, (((1,), (1,)), ((), ())), preferred_element_type=jnp.float32
    )


def kernel(
    sizes,
    clip_ids,
    frame_map,
    segments,
    codes,
    weight,
    projected,
    out,
    far_codes,
    all_codes,
    action,
    bias,
    own,
    spatial,
    got,
    done,
    back,
    result,
    far_send,
    far_recv,
    near_send,
    near_recv,
    code_sem,
    own_sem,
    send_sem,
    recv_sem,
    back_send,
    back_recv,
    out_sem,
):
    clips, group, frames, patches, width = sizes
    near = clips // FAR
    share = patches // group
    slots = group * frames
    rows = slots * share
    wide = HEADS * E
    chunks = width // wide
    scale = 1.0 / E**0.5
    clip = lax.axis_index("dp")
    me = lax.axis_index("frame")
    mp = lax.axis_index("mp")
    my_far, my_near = clip // near, lax.rem(clip, near)
    core = lax.rem(me, 2)

    def far_peer(j):
        return lax.rem(my_far + j, FAR)

    def near_peer(j):
        return lax.rem(my_near + j, near)

    def peer_of(j):
        step = jnp.where(core == 0, j, group - j)
        return jnp.bitwise_xor(me, step)

    barrier = pltpu.get_barrier_semaphore()
    for j in range(1, group):
        pl.semaphore_signal(
            barrier, inc=1, device_id=(clip, peer_of(j), mp), device_id_type=MESH
        )
    for j in range(1, FAR):
        pl.semaphore_signal(
            barrier,
            inc=1,
            device_id=(far_peer(j) * near + my_near, me, mp),
            device_id_type=MESH,
        )
    for j in range(1, near):
        pl.semaphore_signal(
            barrier,
            inc=1,
            device_id=(my_far * near + near_peer(j), me, mp),
            device_id_type=MESH,
        )

    own_code = pltpu.make_async_copy(codes.at[0], far_codes.at[my_far], code_sem.at[0])
    own_code.start()
    own_in = pltpu.make_async_copy(projected.at[0:3, 0], own, own_sem)
    own_in.start()
    pl.semaphore_wait(barrier, group - 1 + FAR - 1 + near - 1)

    def far_copy(j):
        return pltpu.make_async_remote_copy(
            src_ref=codes.at[0],
            dst_ref=far_codes.at[my_far],
            send_sem=far_send.at[j],
            recv_sem=far_recv.at[j],
            device_id=(far_peer(j) * near + my_near, me, mp),
            device_id_type=MESH,
        )

    for j in range(1, FAR):
        far_copy(j).start()

    def part(ref, owner, chunk):
        columns = pl.ds(pl.multiple_of(chunk * wide, wide), wide)
        rows_of = pl.ds(pl.multiple_of(owner * share, share), share)
        return ref.at[3:6, 0, :, rows_of, columns]

    def exchange(chunk, j):
        peer = peer_of(j)
        return pltpu.make_async_remote_copy(
            src_ref=part(projected, peer, chunk),
            dst_ref=got.at[chunk, me],
            send_sem=send_sem.at[chunk, j],
            recv_sem=recv_sem.at[chunk, j],
            device_id=(clip, peer, mp),
            device_id_type=MESH,
        )

    def keep(chunk):
        return pltpu.make_async_copy(
            part(projected, me, chunk), got.at[chunk, me], recv_sem.at[chunk, 0]
        )

    def start_chunk(chunk, carry):
        for j in range(1, group):
            exchange(chunk, j).start()
        keep(chunk).start()
        return carry

    lax.fori_loop(0, chunks, start_chunk, 0)

    for j in range(1, FAR):
        far_copy(j).wait_recv()
    own_code.wait()

    def near_copy(j):
        return pltpu.make_async_remote_copy(
            src_ref=far_codes,
            dst_ref=all_codes.at[my_near],
            send_sem=near_send.at[j],
            recv_sem=near_recv.at[j],
            device_id=(my_far * near + near_peer(j), me, mp),
            device_id_type=MESH,
        )

    for j in range(1, near):
        near_copy(j).start()
    near_own = pltpu.make_async_copy(far_codes, all_codes.at[my_near], code_sem.at[1])
    near_own.start()

    row = lax.broadcasted_iota(jnp.int32, (rows, rows), 0)
    column = lax.broadcasted_iota(jnp.int32, (rows, rows), 1)
    row_time = jnp.zeros((rows, 1), jnp.int32)
    row_part = jnp.zeros((rows, 1), jnp.int32)
    col_time = jnp.zeros((1, rows), jnp.int32)
    col_part = jnp.zeros((1, rows), jnp.int32)
    row_slot = lax.broadcasted_iota(jnp.int32, (rows, 1), 0) // share
    col_slot = lax.broadcasted_iota(jnp.int32, (1, rows), 1) // share
    for s in range(slots):
        time = frame_map[s]
        episode = segments[0, time]
        row_time = jnp.where(row_slot == s, time, row_time)
        row_part = jnp.where(row_slot == s, episode, row_part)
        col_time = jnp.where(col_slot == s, time, col_time)
        col_part = jnp.where(col_slot == s, episode, col_part)
    allowed = (
        (lax.rem(row, share) == lax.rem(column, share))
        & (col_time <= row_time)
        & (col_part == row_part)
    )
    bias[...] = jnp.where(allowed, 0.0, -1e30)

    own_in.wait()

    def one_head(head, carry):
        lanes = pl.ds(pl.multiple_of(head * E, E), E)
        for f in range(frames):
            probs = softmax(scores_of(own[0, f, :, lanes], own[1, f, :, lanes]) * scale)
            spatial[f, :, lanes] = jnp.dot(
                probs, own[2, f, :, lanes], preferred_element_type=jnp.float32
            ).astype(jnp.bfloat16)
        return carry

    lax.fori_loop(0, width // E, one_head, 0)

    for j in range(1, near):
        near_copy(j).wait_recv()
    near_own.wait()
    by_clip = jnp.zeros(codes.shape[1:], jnp.float32)
    for i in range(clips):
        by_clip = by_clip + jnp.where(
            clip_ids[i] == clip, all_codes[i % near, i // near], 0.0
        )
    slot_of = lax.broadcasted_iota(jnp.int32, (slots, 1), 0)
    time_of = jnp.zeros((slots, 1), jnp.int32)
    for s in range(slots):
        time_of = jnp.where(slot_of == s, frame_map[s], time_of)
    by_slot = jnp.zeros(by_clip.shape, jnp.float32)
    for t in range(slots):
        by_slot = by_slot + jnp.where(time_of == t, by_clip[t : t + 1], 0.0)
    action[...] = jnp.dot(
        by_slot,
        weight[...],
        precision=lax.Precision.HIGHEST,
        preferred_element_type=jnp.float32,
    )

    def give(chunk, j):
        peer = peer_of(j)
        return pltpu.make_async_remote_copy(
            src_ref=done.at[chunk, peer],
            dst_ref=back.at[chunk, me],
            send_sem=back_send.at[chunk, j],
            recv_sem=back_recv.at[chunk, j],
            device_id=(clip, peer, mp),
            device_id_type=MESH,
        )

    def give_self(chunk):
        return pltpu.make_async_copy(
            done.at[chunk, me], back.at[chunk, me], back_recv.at[chunk, 0]
        )

    def attend(chunk, carry):
        for j in range(1, group):
            exchange(chunk, j).wait_recv()
        keep(chunk).wait()
        for h in range(HEADS):
            lanes = slice(h * E, (h + 1) * E)
            q = got[chunk, :, 0, :, :, lanes].reshape(rows, E)
            k = got[chunk, :, 1, :, :, lanes].reshape(rows, E)
            raw = got[chunk, :, 2, :, :, lanes].reshape(slots, share, E)
            added = action[:, pl.ds(pl.multiple_of(chunk * wide + h * E, E), E)]
            v = (raw.astype(jnp.float32) + added[:, None, :]).astype(jnp.bfloat16)
            probs = softmax(scores_of(q, k) * scale + bias[...])
            mixed = jnp.dot(
                probs, v.reshape(rows, E), preferred_element_type=jnp.float32
            ).astype(jnp.bfloat16)
            done[chunk, :, :, :, lanes] = mixed.reshape(group, frames, share, E)
        for j in range(1, group):
            give(chunk, j).start()
        give_self(chunk).start()
        return carry

    lax.fori_loop(0, chunks, attend, 0)

    def write(chunk):
        columns = pl.ds(pl.multiple_of(chunk * wide, wide), wide)
        return pltpu.make_async_copy(
            result.at[chunk], out.at[0, :, :, columns], out_sem.at[chunk]
        )

    def finish(chunk, carry):
        for j in range(1, group):
            give(chunk, j).wait_recv()
        give_self(chunk).wait()
        columns = pl.ds(pl.multiple_of(chunk * wide, wide), wide)
        for f in range(frames):
            temporal = back[chunk, :, f].reshape(patches, wide).astype(jnp.float32)
            result[chunk, f] = (
                spatial[f, :, columns].astype(jnp.float32) + temporal
            ).astype(jnp.bfloat16)
        write(chunk).start()
        return carry

    lax.fori_loop(0, chunks, finish, 0)

    def drain(chunk, carry):
        for j in range(1, group):
            exchange(chunk, j).wait_send()
            give(chunk, j).wait_send()
        write(chunk).wait()
        return carry

    lax.fori_loop(0, chunks, drain, 0)
    for j in range(1, FAR):
        far_copy(j).wait_send()
    for j in range(1, near):
        near_copy(j).wait_send()


def solution(mesh):
    clips, group = mesh.shape["dp"], mesh.shape["frame"]

    def local(projected, codes, weight, clip_ids, frame_map, segments):
        _, _, frames, patches, width = projected.shape
        near = clips // FAR
        share = patches // group
        slots = group * frames
        rows = slots * share
        wide = HEADS * E
        chunks = width // wide
        smem = pl.BlockSpec(memory_space=pltpu.SMEM)
        vmem = pl.BlockSpec(memory_space=pltpu.VMEM)
        dma = pltpu.SemaphoreType.DMA
        bf16, f32 = jnp.bfloat16, jnp.float32
        return pl.pallas_call(
            functools.partial(kernel, (clips, group, frames, patches, width)),
            out_shape=jax.ShapeDtypeStruct((1, frames, patches, width), bf16),
            in_specs=[smem, smem, smem, vmem, vmem, pl.BlockSpec(memory_space=pl.ANY)],
            out_specs=pl.BlockSpec(memory_space=pl.ANY),
            scratch_shapes=[
                pltpu.VMEM((FAR, *codes.shape[1:]), f32),
                pltpu.VMEM((near, FAR, *codes.shape[1:]), f32),
                pltpu.VMEM((slots, width), f32),
                pltpu.VMEM((rows, rows), f32),
                pltpu.VMEM((3, frames, patches, width), bf16),
                pltpu.VMEM((frames, patches, width), bf16),
                pltpu.VMEM((chunks, group, 3, frames, share, wide), bf16),
                pltpu.VMEM((chunks, group, frames, share, wide), bf16),
                pltpu.VMEM((chunks, group, frames, share, wide), bf16),
                pltpu.VMEM((chunks, frames, patches, wide), bf16),
                dma((FAR,)),
                dma((FAR,)),
                dma((near,)),
                dma((near,)),
                dma((2,)),
                dma(()),
                dma((chunks, group)),
                dma((chunks, group)),
                dma((chunks, group)),
                dma((chunks, group)),
                dma((chunks,)),
            ],
            compiler_params=pltpu.CompilerParams(
                collective_id=0,
                has_side_effects=True,
                vmem_limit_bytes=67_043_328,
            ),
        )(clip_ids, frame_map, segments, codes, weight, projected)

    return jax.shard_map(
        local,
        mesh=mesh,
        in_specs=(
            P(None, "dp", "frame", None, "mp"),
            P("dp", None, None),
            P(None, "mp"),
            P(),
            P(),
            P("dp", None),
        ),
        out_specs=P("dp", "frame", None, "mp"),
        check_vma=False,
    )
```

time: 184 us -> 79.4 us (0.43)
  Pallas kernels: 0 us -> 77.2 us
  blocking collectives: 74.7 us -> 0 us
  waiting for transfers between devices: 58.4 us -> 0 us
  starting transfers between devices: 20.9 us -> 0 us
  local copies, waits for them, and re-layouts: 21.5 us -> 1.97 us
  matrix products: 6.48 us -> 0 us
    pallas_call x0 -> x1, Pallas kernels: none -> 77.2 us  [local(): pl.pallas_call(functools.partial(kernel, (clips, group, frames, patches,...]
    all_gather x1 -> x0, blocking collectives: 74.7 us -> none  [local(): all_codes = lax.all_gather(codes, 'dp', axis=0, tiled=True)]
    all_to_all x2 -> x0, waiting for transfers between devices: 58.4 us -> none  [the longest x1 45 us: local(): lax.all_to_all(temporal_in, 'frame', split_axis=3, concat_axis=2, tiled=T...]
    all_to_all x2 -> x0, starting transfers between devices: 20.9 us -> none  [the longest x1 16.4 us: local(): lax.all_to_all(temporal_in, 'frame', split_axis=3, concat_axis=2, tiled=T...]
    slice x6 -> x0, local copies, waits for them, and re-layouts: 6.98 us -> none  [the longest x1 3.39 us: local(): reshaped_rows[1]]
    dot_general x7 -> x0, matrix products: 5.89 us -> none  [the longest x1 2.28 us: local(): jnp.einsum('cfhpq,cfqhe->cfphe', probs, reshaped_rows[2], preferred_eleme...]
    another operation x1 -> x0, local copies, waits for them, and re-layouts: 4.72 us -> none  [local(): temporal_in = jnp.stack([reshaped_rows[3], reshaped_rows[4], values_t])]
    unnamed x19 -> x1, local copies, waits for them, and re-layouts: 5.8 us -> 1.97 us
  transfers between devices with their start and end apart: 2 -> 0, of which waited for: 2 -> 0; matrix products, arithmetic and copies ran while one was open for 2% -> 0% of each run, Pallas kernels for 0% -> 0%
where the time goes in v1:
time: 79.4 us; the launch traced here: 79.2 us
  Pallas kernels  77.2 us (97%)
  local copies, waits for them, and re-layouts  1.97 us (2%)
    pallas_call x1, Pallas kernels, local(): pl.pallas_call(functools.partial(kernel, (clips, group, frames, patches,...  77.2 us
    unnamed x1, local copies, waits for them, and re-layouts  1.97 us

profile of v1, /device:TPU:1, one launch (start us, length us, event | category | flops | bytes accessed | tf_op | source)
XLA Modules:
  0.0 79.2 jit_solution(129127128572566185)
XLA Ops:
  0.0 77.2 %shard_map.64 = bf16[1,2,128,1280]{3,2,1,0:T(8,128)(2,1)} custom-call(s32[24]{0:T(128)} %clip_ids.1, s32[16]{0:T(128)} %frame_map.1, s32[1,16]{1,0:T(1,128)} %segments.1, f32[1,16,32]{2,1,0:T(8,128)} %codes.1, f32[32,1280]{1,0:T(8,128)} %weight.1, bf16[6,1,2,128,1280]{4,3,2,1,0:T(8,128)(2,1)} %projected.1), custom_call_target="tpu_custom_call" | custom-call | tf_op jit(solution)/shard_map/pallas_call | solution.py:316
  77.2 2.0 %copy.8 = bf16[1,2,128,1280]{3,2,1,0:T(8,128)(2,1)} copy(bf16[1,2,128,1280]{3,2,1,0:T(8,128)(2,1)} %shard_map.64) | data formatting | bytes 1310720

commit v2 on v1

v2 whole, which is shorter than its diff:
```python
import functools

import jax
import jax.numpy as jnp
from jax import lax
from jax.experimental import pallas as pl
from jax.experimental.pallas import tpu as pltpu
from jax.sharding import PartitionSpec as P

MESH = pl.DeviceIdType.MESH
E = 128
FAR = 3
CORES = 2
SIZES = (5, 3, 2)
MOVES = 4


def softmax(scores):
    peak = jnp.max(scores, axis=-1, keepdims=True)
    weights = jnp.exp(scores - peak)
    return (weights / jnp.sum(weights, axis=-1, keepdims=True)).astype(jnp.bfloat16)


def scores_of(q, k):
    return lax.dot_general(
        q, k, (((1,), (1,)), ((), ())), preferred_element_type=jnp.float32
    )


def kernel(
    sizes,
    clip_ids_in,
    frame_map_in,
    segments_in,
    codes_in,
    weight_in,
    projected,
    out,
    clip_ids,
    frame_map,
    segments,
    codes,
    weight,
    far_codes,
    all_codes,
    action,
    bias,
    own,
    got,
    done,
    back,
    result,
    out_sem,
    small_sem,
    far_send,
    far_recv,
    far_hello,
    hello,
    near_hello,
    near_send,
    near_recv,
    code_sem,
    own_sem,
    send_sem,
    recv_sem,
    back_send,
    back_recv,
):
    clips, group, frames, patches, width = sizes
    near = clips // FAR
    share = patches // group
    slots = group * frames
    rows = slots * share
    chunks = len(SIZES)
    chips = group // CORES
    starts = [sum(SIZES[:c]) for c in range(chunks)]
    scale = 1.0 / E**0.5
    clip = lax.axis_index("dp")
    me = lax.axis_index("frame")
    mp = lax.axis_index("mp")
    my_far, my_near = clip // near, lax.rem(clip, near)
    chip, core = me // CORES, lax.rem(me, CORES)

    def peer_of(j):
        return jnp.bitwise_xor(me, j)

    def at_frame(peer):
        return (clip, peer, mp)

    def at_near(peer):
        return (my_far * near + peer, me, mp)

    def at_far(part, chip_there):
        return (part * near + my_near, chip_there * CORES + core, mp)

    ends = (chips - 1, 0)
    there = (lax.rem(my_far + 1, FAR), lax.rem(my_far + FAR - 1, FAR))

    small = [
        pltpu.make_async_copy(a, b, small_sem.at[i])
        for i, (a, b) in enumerate(
            (
                (clip_ids_in, clip_ids),
                (frame_map_in, frame_map),
                (segments_in, segments),
                (codes_in, codes),
                (weight_in, weight),
            )
        )
    ]
    own_in = pltpu.make_async_copy(projected.at[0:3, 0], own, own_sem)

    barrier = pltpu.get_barrier_semaphore()
    for peer in range(1, group):
        @pl.when(peer > me)
        def _():
            pl.semaphore_signal(
                barrier, inc=1, device_id=at_frame(peer), device_id_type=MESH
            )

    for peer in range(1, near):
        @pl.when(peer > my_near)
        def _():
            pl.semaphore_signal(
                barrier, inc=1, device_id=at_near(peer), device_id_type=MESH
            )

    for side in range(2):
        @pl.when((chip == ends[side]) & (there[side] > my_far))
        def _():
            for z in range(chips):
                pl.semaphore_signal(
                    barrier,
                    inc=1,
                    device_id=at_far(there[side], z),
                    device_id_type=MESH,
                )

        @pl.when(there[side] > my_far)
        def _():
            pl.semaphore_signal(
                barrier,
                inc=1,
                device_id=at_far(there[side], ends[1 - side]),
                device_id_type=MESH,
            )

    for copy in small:
        copy.start()
    own_in.start()
    heard = me + my_near
    for side in range(2):
        earlier = there[side] < my_far
        heard = heard + jnp.where(earlier, 1, 0)
        heard = heard + jnp.where(earlier & (chip == ends[side]), chips, 0)

    @pl.when(heard > 0)
    def _():
        pl.semaphore_wait(barrier, heard)


    def lanes_of(chunk):
        return slice(starts[chunk] * E, (starts[chunk] + SIZES[chunk]) * E)

    def part(owner, chunk):
        mine = pl.ds(pl.multiple_of(owner * share, share), share)
        return projected.at[3:6, 0, :, mine, lanes_of(chunk)]

    def exchange(chunk, peer):
        return pltpu.make_async_remote_copy(
            src_ref=part(peer, chunk),
            dst_ref=got.at[me, :, :, :, lanes_of(chunk)],
            send_sem=send_sem.at[chunk, peer],
            recv_sem=recv_sem.at[chunk, me],
            device_id=at_frame(peer),
            device_id_type=MESH,
        )

    def got_from(chunk, peer):
        return pltpu.make_async_remote_copy(
            src_ref=part(peer, chunk),
            dst_ref=got.at[peer, :, :, :, lanes_of(chunk)],
            send_sem=send_sem.at[chunk, peer],
            recv_sem=recv_sem.at[chunk, peer],
            device_id=at_frame(peer),
            device_id_type=MESH,
        )

    def keep(chunk):
        return pltpu.make_async_copy(
            part(me, chunk),
            got.at[me, :, :, :, lanes_of(chunk)],
            recv_sem.at[chunk, me],
        )

    for j in range(1, group):
        @pl.when(peer_of(j) < me)
        def _():
            exchange(0, peer_of(j)).start()
            pl.semaphore_signal(
                hello.at[me], inc=1, device_id=at_frame(peer_of(j)), device_id_type=MESH
            )

    for peer in range(1, group):
        @pl.when(peer > me)
        def _():
            pl.semaphore_wait(hello.at[peer], 1)
            exchange(0, peer).start()

    keep(0).start()
    for chunk in range(1, chunks):
        for j in range(1, group):
            exchange(chunk, peer_of(j)).start()
        keep(chunk).start()

    for peer in range(near - 1):
        @pl.when(peer < my_near)
        def _():
            pl.semaphore_signal(
                near_hello.at[my_near],
                inc=1,
                device_id=at_near(peer),
                device_id_type=MESH,
            )

    for side in range(2):
        @pl.when(there[side] < my_far)
        def _():
            pl.semaphore_signal(
                far_hello,
                inc=1,
                device_id=at_far(there[side], ends[1 - side]),
                device_id_type=MESH,
            )

    for copy in small:
        copy.wait()

    def far_copy(side, z):
        return pltpu.make_async_remote_copy(
            src_ref=codes.at[0],
            dst_ref=far_codes.at[my_far],
            send_sem=far_send.at[side, z],
            recv_sem=far_recv.at[side],
            device_id=at_far(there[side], z),
            device_id_type=MESH,
        )

    def far_start(side, when):
        @pl.when((chip == ends[side]) & when)
        def _():
            for z in range(chips):
                far_copy(side, z).start()

    for side in range(2):
        far_start(side, there[side] < my_far)
    own_code = pltpu.make_async_copy(codes.at[0], far_codes.at[my_far], code_sem.at[0])
    own_code.start()

    row = lax.broadcasted_iota(jnp.int32, (rows, rows), 0)
    column = lax.broadcasted_iota(jnp.int32, (rows, rows), 1)
    row_time = jnp.zeros((rows, 1), jnp.int32)
    row_part = jnp.zeros((rows, 1), jnp.int32)
    col_time = jnp.zeros((1, rows), jnp.int32)
    col_part = jnp.zeros((1, rows), jnp.int32)
    row_slot = lax.broadcasted_iota(jnp.int32, (rows, 1), 0) // share
    col_slot = lax.broadcasted_iota(jnp.int32, (1, rows), 1) // share
    for s in range(slots):
        time = frame_map[s]
        episode = segments[0, time]
        row_time = jnp.where(row_slot == s, time, row_time)
        row_part = jnp.where(row_slot == s, episode, row_part)
        col_time = jnp.where(col_slot == s, time, col_time)
        col_part = jnp.where(col_slot == s, episode, col_part)
    allowed = (
        (lax.rem(row, share) == lax.rem(column, share))
        & (col_time <= row_time)
        & (col_part == row_part)
    )
    bias[...] = jnp.where(allowed, 0.0, -1e30)

    own_in.wait()

    def one_head(head, carry):
        lanes = pl.ds(pl.multiple_of(head * E, E), E)
        for f in range(frames):
            probs = softmax(scores_of(own[0, f, :, lanes], own[1, f, :, lanes]) * scale)
            result[f, :, lanes] = jnp.dot(
                probs, own[2, f, :, lanes], preferred_element_type=jnp.float32
            ).astype(jnp.bfloat16)
        return carry

    lax.fori_loop(0, width // E, one_head, 0)

    for side in range(2):
        @pl.when((chip == ends[side]) & (there[side] > my_far))
        def _():
            pl.semaphore_wait(far_hello, chips)

        far_start(side, there[side] > my_far)
    own_code.wait()
    for side in range(2):
        pltpu.make_async_remote_copy(
            src_ref=codes.at[0],
            dst_ref=far_codes.at[there[1 - side]],
            send_sem=far_send.at[side, 0],
            recv_sem=far_recv.at[side],
            device_id=at_far(there[side], 0),
            device_id_type=MESH,
        ).wait_recv()

    def near_copy(peer, source):
        return pltpu.make_async_remote_copy(
            src_ref=far_codes,
            dst_ref=all_codes.at[source],
            send_sem=near_send.at[peer],
            recv_sem=near_recv.at[source],
            device_id=at_near(peer),
            device_id_type=MESH,
        )

    for peer in range(near):
        @pl.when(peer < my_near)
        def _():
            near_copy(peer, my_near).start()

    for peer in range(near):
        @pl.when(peer > my_near)
        def _():
            pl.semaphore_wait(near_hello.at[peer], 1)
            near_copy(peer, my_near).start()

    near_own = pltpu.make_async_copy(far_codes, all_codes.at[my_near], code_sem.at[1])
    near_own.start()
    for peer in range(near):
        @pl.when(peer != my_near)
        def _():
            near_copy(peer, peer).wait_recv()

    near_own.wait()

    by_clip = jnp.zeros(codes.shape[1:], jnp.float32)
    for i in range(clips):
        by_clip = by_clip + jnp.where(
            clip_ids[i] == clip, all_codes[i % near, i // near], 0.0
        )
    slot_of = lax.broadcasted_iota(jnp.int32, (slots, 1), 0)
    time_of = jnp.zeros((slots, 1), jnp.int32)
    for s in range(slots):
        time_of = jnp.where(slot_of == s, frame_map[s], time_of)
    by_slot = jnp.zeros(by_clip.shape, jnp.float32)
    for t in range(slots):
        by_slot = by_slot + jnp.where(time_of == t, by_clip[t : t + 1], 0.0)
    action[...] = jnp.dot(
        by_slot,
        weight[...],
        precision=lax.Precision.HIGHEST,
        preferred_element_type=jnp.float32,
    )

    def give(chunk, j):
        peer = peer_of(j)
        return pltpu.make_async_remote_copy(
            src_ref=done.at[peer, :, :, lanes_of(chunk)],
            dst_ref=back.at[me, :, :, lanes_of(chunk)],
            send_sem=back_send.at[chunk, j],
            recv_sem=back_recv.at[chunk, j],
            device_id=at_frame(peer),
            device_id_type=MESH,
        )

    def give_self(chunk):
        return pltpu.make_async_copy(
            done.at[me, :, :, lanes_of(chunk)],
            back.at[me, :, :, lanes_of(chunk)],
            back_recv.at[chunk, 0],
        )

    def attend(head, carry):
        lanes = pl.ds(pl.multiple_of(head * E, E), E)
        q = got[:, 0, :, :, lanes].reshape(rows, E)
        k = got[:, 1, :, :, lanes].reshape(rows, E)
        raw = got[:, 2, :, :, lanes].reshape(slots, share, E)
        added = action[:, lanes]
        v = (raw.astype(jnp.float32) + added[:, None, :]).astype(jnp.bfloat16)
        probs = softmax(scores_of(q, k) * scale + bias[...])
        mixed = jnp.dot(
            probs, v.reshape(rows, E), preferred_element_type=jnp.float32
        ).astype(jnp.bfloat16)
        done[:, :, :, lanes] = mixed.reshape(group, frames, share, E)
        return carry

    for chunk in range(chunks):
        for j in range(1, group):
            got_from(chunk, peer_of(j)).wait_recv()
        keep(chunk).wait()
        lax.fori_loop(starts[chunk], starts[chunk] + SIZES[chunk], attend, 0)
        for j in range(1, group):
            give(chunk, j).start()
        give_self(chunk).start()

    def write(chunk):
        lanes = lanes_of(chunk)
        return pltpu.make_async_copy(
            result.at[:, :, lanes], out.at[0, :, :, lanes], out_sem.at[chunk]
        )

    for chunk in range(chunks):
        for j in range(1, group):
            give(chunk, j).wait_recv()
        give_self(chunk).wait()
        lanes = lanes_of(chunk)
        for f in range(frames):
            temporal = back[:, f, :, lanes].astype(jnp.float32)
            result[f, :, lanes] = (
                result[f, :, lanes].astype(jnp.float32)
                + temporal.reshape(patches, SIZES[chunk] * E)
            ).astype(jnp.bfloat16)
        write(chunk).start()

    for chunk in range(chunks):
        for j in range(1, group):
            exchange(chunk, peer_of(j)).wait_send()
            give(chunk, j).wait_send()
        write(chunk).wait()
    for side in range(2):
        @pl.when(chip == ends[side])
        def _():
            for z in range(chips):
                far_copy(side, z).wait_send()
    for peer in range(near):
        @pl.when(peer != my_near)
        def _():
            near_copy(peer, my_near).wait_send()


def move(source, out, sems):
    step = source.shape[2] // MOVES
    copies = [
        pltpu.make_async_copy(
            source.at[0, f, i * step : (i + 1) * step],
            out.at[0, f, i * step : (i + 1) * step],
            sems.at[f, i],
        )
        for f in range(source.shape[1])
        for i in range(MOVES)
    ]
    for copy in copies:
        copy.start()
    for copy in copies:
        copy.wait()


def solution(mesh):
    clips, group = mesh.shape["dp"], mesh.shape["frame"]

    def local(projected, codes, weight, clip_ids, frame_map, segments):
        _, _, frames, patches, width = projected.shape
        near = clips // FAR
        share = patches // group
        slots = group * frames
        rows = slots * share
        chunks = len(SIZES)
        anywhere = pl.BlockSpec(memory_space=pl.ANY)
        dma = pltpu.SemaphoreType.DMA
        bf16, f32 = jnp.bfloat16, jnp.float32
        shape = jax.ShapeDtypeStruct((1, frames, patches, width), bf16)
        mixed = pl.pallas_call(
            functools.partial(kernel, (clips, group, frames, patches, width)),
            out_shape=pltpu.VMEM(shape.shape, bf16),
            in_specs=[anywhere] * 6,
            out_specs=anywhere,
            scratch_shapes=[
                pltpu.SMEM(clip_ids.shape, clip_ids.dtype),
                pltpu.SMEM(frame_map.shape, frame_map.dtype),
                pltpu.SMEM(segments.shape, segments.dtype),
                pltpu.VMEM(codes.shape, f32),
                pltpu.VMEM(weight.shape, f32),
                pltpu.VMEM((FAR, *codes.shape[1:]), f32),
                pltpu.VMEM((near, FAR, *codes.shape[1:]), f32),
                pltpu.VMEM((slots, width), f32),
                pltpu.VMEM((rows, rows), f32),
                pltpu.VMEM((3, frames, patches, width), bf16),
                pltpu.VMEM((group, 3, frames, share, width), bf16),
                pltpu.VMEM((group, frames, share, width), bf16),
                pltpu.VMEM((group, frames, share, width), bf16),
                pltpu.VMEM((frames, patches, width), bf16),
                dma((chunks,)),
                dma((5,)),
                dma((2, group // CORES)),
                dma((2,)),
                pltpu.SemaphoreType.REGULAR,
                pltpu.SemaphoreType.REGULAR((group,)),
                pltpu.SemaphoreType.REGULAR((near,)),
                dma((near,)),
                dma((near,)),
                dma((2,)),
                dma(()),
                dma((chunks, group)),
                dma((chunks, group)),
                dma((chunks, group)),
                dma((chunks, group)),
            ],
            compiler_params=pltpu.CompilerParams(
                collective_id=0,
                has_side_effects=True,
                vmem_limit_bytes=64_000_000,
            ),
        )(
            *(
                pltpu.with_memory_space_constraint(x, pltpu.HBM)
                for x in (clip_ids, frame_map, segments, codes, weight, projected)
            )
        )
        return pl.pallas_call(
            move,
            out_shape=shape,
            in_specs=[anywhere],
            out_specs=anywhere,
            scratch_shapes=[dma((frames, MOVES))],
        )(pltpu.with_memory_space_constraint(mixed, pltpu.VMEM))

    return jax.shard_map(
        local,
        mesh=mesh,
        in_specs=(
            P(None, "dp", "frame", None, "mp"),
            P("dp", None, None),
            P(None, "mp"),
            P(),
            P(),
            P("dp", None),
        ),
        out_specs=P("dp", "frame", None, "mp"),
        check_vma=False,
    )
```

time: 79.4 us -> 73.6 us (0.927)
  Pallas kernels: 77.2 us -> 73.5 us
  local copies, waits for them, and re-layouts: 1.97 us -> 0 us
    pallas_call x1, Pallas kernels: 77.2 us -> 72.6 us  [local(): pl.pallas_call(functools.partial(kernel, (clips, group, frames, patches,...]
    unnamed x1 -> x0, local copies, waits for them, and re-layouts: 1.97 us -> none
    pallas_call x0 -> x1, Pallas kernels: none -> 0.9 us  [local(): pl.pallas_call(move, out_shape=shape, in_specs=[anywhere], out_specs=anyw...]
where the time goes in v2:
time: 73.6 us; the launch traced here: 73.5 us
  Pallas kernels  73.5 us (100%)
    pallas_call x1, Pallas kernels, local(): pl.pallas_call(functools.partial(kernel, (clips, group, frames, patches,...  72.6 us

profile of v2, /device:TPU:1, one launch (start us, length us, event | category | flops | bytes accessed | tf_op | source)
XLA Modules:
  0.0 73.5 jit_solution(2575030779687992816)
XLA Ops:
  0.0 72.6 %shard_map.64.source = bf16[1,2,128,1280]{3,2,1,0:T(8,128)(2,1)S(1)} custom-call(s32[24]{0:T(128)} %clip_ids_in.1, s32[16]{0:T(128)} %frame_map_in.1, s32[1,16]{1,0:T(1,128)} %segments_in.1, f32[1,16,32]{2,1,0:T(8,128)} %codes_in.1, f32[32,1280]{1,0:T(8,128)} %weight_in.1, bf16[6,1,2,128,1280]{4,3,2,1,0:T(8,128)(2,1)} %projected.1), custom_call_target="tpu_custom_call" | custom-call | tf_op jit(solution)/shard_map/pallas_call | solution.py:468
  72.6 0.9 %shard_map.65 = bf16[1,2,128,1280]{3,2,1,0:T(8,128)(2,1)} custom-call(bf16[1,2,128,1280]{3,2,1,0:T(8,128)(2,1)S(1)} %shard_map.64.source), custom_call_target="tpu_custom_call" | custom-call | tf_op jit(solution)/shard_map/pallas_call | solution.py:515

commit v3 on v2

--- a/solution.py
+++ b/solution.py
@@ -49,8 +49,6 @@
     got,
     done,
     back,
-    result,
-    out_sem,
     small_sem,
     far_send,
     far_recv,
@@ -110,16 +108,28 @@
     ]
     own_in = pltpu.make_async_copy(projected.at[0:3, 0], own, own_sem)
 
+    corner = (my_far == 0) & (mp == 0)
+    shift = jnp.where(corner & (my_near == 0), 1, 0)
+    near_shift = jnp.where(corner & (me == 0), 1, 0)
+
+    def rank(peer):
+        return lax.rem(peer + group - shift, group)
+
+    def near_rank(peer):
+        return lax.rem(peer + near - near_shift, near)
+
+    my_rank, my_near_rank = rank(me), near_rank(my_near)
+
     barrier = pltpu.get_barrier_semaphore()
-    for peer in range(1, group):
-        @pl.when(peer > me)
+    for peer in range(group):
+        @pl.when(rank(peer) > my_rank)
         def _():
             pl.semaphore_signal(
                 barrier, inc=1, device_id=at_frame(peer), device_id_type=MESH
             )
 
-    for peer in range(1, near):
-        @pl.when(peer > my_near)
+    for peer in range(near):
+        @pl.when(near_rank(peer) > my_near_rank)
         def _():
             pl.semaphore_signal(
                 barrier, inc=1, device_id=at_near(peer), device_id_type=MESH
@@ -148,7 +158,7 @@
     for copy in small:
         copy.start()
     own_in.start()
-    heard = me + my_near
+    heard = my_rank + my_near_rank
     for side in range(2):
         earlier = there[side] < my_far
         heard = heard + jnp.where(earlier, 1, 0)
@@ -194,15 +204,15 @@
         )
 
     for j in range(1, group):
-        @pl.when(peer_of(j) < me)
+        @pl.when(rank(peer_of(j)) < my_rank)
         def _():
             exchange(0, peer_of(j)).start()
             pl.semaphore_signal(
                 hello.at[me], inc=1, device_id=at_frame(peer_of(j)), device_id_type=MESH
             )
 
-    for peer in range(1, group):
-        @pl.when(peer > me)
+    for peer in (*range(1, group), 0):
+        @pl.when(rank(peer) > my_rank)
         def _():
             pl.semaphore_wait(hello.at[peer], 1)
             exchange(0, peer).start()
@@ -213,8 +223,8 @@
             exchange(chunk, peer_of(j)).start()
         keep(chunk).start()
 
-    for peer in range(near - 1):
-        @pl.when(peer < my_near)
+    for peer in range(near):
+        @pl.when(near_rank(peer) < my_near_rank)
         def _():
             pl.semaphore_signal(
                 near_hello.at[my_near],
@@ -285,7 +295,7 @@
         lanes = pl.ds(pl.multiple_of(head * E, E), E)
         for f in range(frames):
             probs = softmax(scores_of(own[0, f, :, lanes], own[1, f, :, lanes]) * scale)
-            result[f, :, lanes] = jnp.dot(
+            out[0, f, :, lanes] = jnp.dot(
                 probs, own[2, f, :, lanes], preferred_element_type=jnp.float32
             ).astype(jnp.bfloat16)
         return carry
@@ -320,12 +330,12 @@
         )
 
     for peer in range(near):
-        @pl.when(peer < my_near)
+        @pl.when(near_rank(peer) < my_near_rank)
         def _():
             near_copy(peer, my_near).start()
 
-    for peer in range(near):
-        @pl.when(peer > my_near)
+    for peer in (*range(1, near), 0):
+        @pl.when(near_rank(peer) > my_near_rank)
         def _():
             pl.semaphore_wait(near_hello.at[peer], 1)
             near_copy(peer, my_near).start()
@@ -399,12 +409,6 @@
             give(chunk, j).start()
         give_self(chunk).start()
 
-    def write(chunk):
-        lanes = lanes_of(chunk)
-        return pltpu.make_async_copy(
-            result.at[:, :, lanes], out.at[0, :, :, lanes], out_sem.at[chunk]
-        )
-
     for chunk in range(chunks):
         for j in range(1, group):
             give(chunk, j).wait_recv()
@@ -412,17 +416,15 @@
         lanes = lanes_of(chunk)
         for f in range(frames):
             temporal = back[:, f, :, lanes].astype(jnp.float32)
-            result[f, :, lanes] = (
-                result[f, :, lanes].astype(jnp.float32)
+            out[0, f, :, lanes] = (
+                out[0, f, :, lanes].astype(jnp.float32)
                 + temporal.reshape(patches, SIZES[chunk] * E)
             ).astype(jnp.bfloat16)
-        write(chunk).start()
 
     for chunk in range(chunks):
         for j in range(1, group):
             exchange(chunk, peer_of(j)).wait_send()
             give(chunk, j).wait_send()
-        write(chunk).wait()
     for side in range(2):
         @pl.when(chip == ends[side])
         def _():
@@ -469,7 +471,7 @@
             functools.partial(kernel, (clips, group, frames, patches, width)),
             out_shape=pltpu.VMEM(shape.shape, bf16),
             in_specs=[anywhere] * 6,
-            out_specs=anywhere,
+            out_specs=pl.BlockSpec(memory_space=pltpu.VMEM),
             scratch_shapes=[
                 pltpu.SMEM(clip_ids.shape, clip_ids.dtype),
                 pltpu.SMEM(frame_map.shape, frame_map.dtype),
@@ -484,8 +486,6 @@
                 pltpu.VMEM((group, 3, frames, share, width), bf16),
                 pltpu.VMEM((group, frames, share, width), bf16),
                 pltpu.VMEM((group, frames, share, width), bf16),
-                pltpu.VMEM((frames, patches, width), bf16),
-                dma((chunks,)),
                 dma((5,)),
                 dma((2, group // CORES)),
                 dma((2,)),

time: 73.6 us -> 67.5 us (0.917)
  the two profiles are of different devices: /device:TPU:1 before, /device:TPU:57 now
where the time goes in v3:
time: 67.5 us; the launch traced here: 67.3 us
  Pallas kernels  67.3 us (100%)
    pallas_call x1, Pallas kernels, local(): pl.pallas_call(functools.partial(kernel, (clips, group, frames, patches,...  66.4 us

profile of v3, /device:TPU:57, one launch (start us, length us, event | category | flops | bytes accessed | tf_op | source)
XLA Modules:
  0.0 67.3 jit_solution(174821718293176918)
XLA Ops:
  0.0 66.4 %shard_map.64.source = bf16[1,2,128,1280]{3,2,1,0:T(8,128)(2,1)S(1)} custom-call(s32[24]{0:T(128)} %clip_ids_in.1, s32[16]{0:T(128)} %frame_map_in.1, s32[1,16]{1,0:T(1,128)} %segments_in.1, f32[1,16,32]{2,1,0:T(8,128)} %codes_in.1, f32[32,1280]{1,0:T(8,128)} %weight_in.1, bf16[6,1,2,128,1280]{4,3,2,1,0:T(8,128)(2,1)} %projected.1), custom_call_target="tpu_custom_call" | custom-call | tf_op jit(solution)/shard_map/pallas_call | solution.py:470
  66.4 0.9 %shard_map.65 = bf16[1,2,128,1280]{3,2,1,0:T(8,128)(2,1)} custom-call(bf16[1,2,128,1280]{3,2,1,0:T(8,128)(2,1)S(1)} %shard_map.64.source), custom_call_target="tpu_custom_call" | custom-call | tf_op jit(solution)/shard_map/pallas_call | solution.py:515

commit v4 on v3

--- a/solution.py
+++ b/solution.py
@@ -128,11 +128,12 @@
                 barrier, inc=1, device_id=at_frame(peer), device_id_type=MESH
             )
 
-    for peer in range(near):
-        @pl.when(near_rank(peer) > my_near_rank)
+    beside = (lax.rem(my_near + 1, near), lax.rem(my_near + near - 1, near))
+    for side in range(2):
+        @pl.when(near_rank(beside[side]) > my_near_rank)
         def _():
             pl.semaphore_signal(
-                barrier, inc=1, device_id=at_near(peer), device_id_type=MESH
+                barrier, inc=1, device_id=at_near(beside[side]), device_id_type=MESH
             )
 
     for side in range(2):
@@ -158,8 +159,9 @@
     for copy in small:
         copy.start()
     own_in.start()
-    heard = my_rank + my_near_rank
-    for side in range(2):
+    heard = my_rank
+    for side in range(2):
+        heard = heard + jnp.where(near_rank(beside[side]) < my_near_rank, 1, 0)
         earlier = there[side] < my_far
         heard = heard + jnp.where(earlier, 1, 0)
         heard = heard + jnp.where(earlier & (chip == ends[side]), chips, 0)
@@ -223,13 +225,13 @@
             exchange(chunk, peer_of(j)).start()
         keep(chunk).start()
 
-    for peer in range(near):
-        @pl.when(near_rank(peer) < my_near_rank)
+    for side in range(2):
+        @pl.when(near_rank(beside[side]) < my_near_rank)
         def _():
             pl.semaphore_signal(
-                near_hello.at[my_near],
+                near_hello.at[1 - side],
                 inc=1,
-                device_id=at_near(peer),
+                device_id=at_near(beside[side]),
                 device_id_type=MESH,
             )
 
@@ -319,34 +321,44 @@
             device_id_type=MESH,
         ).wait_recv()
 
-    def near_copy(peer, source):
+    hops = (near // 2, (near - 1) // 2)
+
+    def near_copy(side, hop):
+        source = lax.rem(my_near + (near - hop if side == 0 else hop), near)
+        return pltpu.make_async_remote_copy(
+            src_ref=far_codes if hop == 0 else all_codes.at[source],
+            dst_ref=all_codes.at[source],
+            send_sem=near_send.at[side, hop],
+            recv_sem=near_recv.at[side, hop],
+            device_id=at_near(beside[side]),
+            device_id_type=MESH,
+        )
+
+    def near_arrived(side, hop):
+        source = lax.rem(my_near + (near - hop - 1 if side == 0 else hop + 1), near)
         return pltpu.make_async_remote_copy(
             src_ref=far_codes,
             dst_ref=all_codes.at[source],
-            send_sem=near_send.at[peer],
-            recv_sem=near_recv.at[source],
-            device_id=at_near(peer),
-            device_id_type=MESH,
-        )
-
-    for peer in range(near):
-        @pl.when(near_rank(peer) < my_near_rank)
-        def _():
-            near_copy(peer, my_near).start()
-
-    for peer in (*range(1, near), 0):
-        @pl.when(near_rank(peer) > my_near_rank)
-        def _():
-            pl.semaphore_wait(near_hello.at[peer], 1)
-            near_copy(peer, my_near).start()
-
+            send_sem=near_send.at[side, hop],
+            recv_sem=near_recv.at[side, hop],
+            device_id=at_near(beside[side]),
+            device_id_type=MESH,
+        )
+
+    for side in range(2):
+        @pl.when(near_rank(beside[side]) > my_near_rank)
+        def _():
+            pl.semaphore_wait(near_hello.at[side], 1)
+
+        near_copy(side, 0).start()
     near_own = pltpu.make_async_copy(far_codes, all_codes.at[my_near], code_sem.at[1])
     near_own.start()
-    for peer in range(near):
-        @pl.when(peer != my_near)
-        def _():
-            near_copy(peer, peer).wait_recv()
-
+    for hop in range(hops[0]):
+        for side in range(2):
+            if hop < hops[side]:
+                near_arrived(side, hop).wait_recv()
+            if hop + 1 < hops[side]:
+                near_copy(side, hop + 1).start()
     near_own.wait()
 
     by_clip = jnp.zeros(codes.shape[1:], jnp.float32)
@@ -430,10 +442,9 @@
         def _():
             for z in range(chips):
                 far_copy(side, z).wait_send()
-    for peer in range(near):
-        @pl.when(peer != my_near)
-        def _():
-            near_copy(peer, my_near).wait_send()
+    for side in range(2):
+        for hop in range(hops[side]):
+            near_copy(side, hop).wait_send()
 
 
 def move(source, out, sems):
@@ -491,9 +502,9 @@
                 dma((2,)),
                 pltpu.SemaphoreType.REGULAR,
                 pltpu.SemaphoreType.REGULAR((group,)),
-                pltpu.SemaphoreType.REGULAR((near,)),
-                dma((near,)),
-                dma((near,)),
+                pltpu.SemaphoreType.REGULAR((2,)),
+                dma((2, near // 2)),
+                dma((2, near // 2)),
                 dma((2,)),
                 dma(()),
                 dma((chunks, group)),

time: 67.5 us -> 66.1 us (0.979)
  the two profiles are of different devices: /device:TPU:57 before, /device:TPU:1 now
where the time goes in v4:
time: 66.1 us; the launch traced here: 65.9 us
  Pallas kernels  65.9 us (100%)
    pallas_call x1, Pallas kernels, local(): pl.pallas_call(functools.partial(kernel, (clips, group, frames, patches,...  65 us

profile of v4, /device:TPU:1, one launch (start us, length us, event | category | flops | bytes accessed | tf_op | source)
XLA Modules:
  0.0 65.9 jit_solution(13510980115322859484)
XLA Ops:
  0.0 65.0 %shard_map.64.source = bf16[1,2,128,1280]{3,2,1,0:T(8,128)(2,1)S(1)} custom-call(s32[24]{0:T(128)} %clip_ids_in.1, s32[16]{0:T(128)} %frame_map_in.1, s32[1,16]{1,0:T(1,128)} %segments_in.1, f32[1,16,32]{2,1,0:T(8,128)} %codes_in.1, f32[32,1280]{1,0:T(8,128)} %weight_in.1, bf16[6,1,2,128,1280]{4,3,2,1,0:T(8,128)(2,1)} %projected.1), custom_call_target="tpu_custom_call" | custom-call | tf_op jit(solution)/shard_map/pallas_call | solution.py:481
  65.0 0.9 %shard_map.65 = bf16[1,2,128,1280]{3,2,1,0:T(8,128)(2,1)} custom-call(bf16[1,2,128,1280]{3,2,1,0:T(8,128)(2,1)S(1)} %shard_map.64.source), custom_call_target="tpu_custom_call" | custom-call | tf_op jit(solution)/shard_map/pallas_call | solution.py:526

commit v5 on v4

--- a/solution.py
+++ b/solution.py
@@ -43,6 +43,8 @@
     weight,
     far_codes,
     all_codes,
+    row_out,
+    row_in,
     action,
     bias,
     own,
@@ -52,6 +54,8 @@
     small_sem,
     far_send,
     far_recv,
+    row_send,
+    row_recv,
     far_hello,
     hello,
     near_hello,
@@ -130,16 +134,18 @@
 
     beside = (lax.rem(my_near + 1, near), lax.rem(my_near + near - 1, near))
     for side in range(2):
-        @pl.when(near_rank(beside[side]) > my_near_rank)
+        @pl.when((chip == 0) & (near_rank(beside[side]) > my_near_rank))
         def _():
             pl.semaphore_signal(
                 barrier, inc=1, device_id=at_near(beside[side]), device_id_type=MESH
             )
 
+    reach = (1, chips)
+    reached = (chip >= 0, chip == 0)
     for side in range(2):
         @pl.when((chip == ends[side]) & (there[side] > my_far))
         def _():
-            for z in range(chips):
+            for z in range(reach[side]):
                 pl.semaphore_signal(
                     barrier,
                     inc=1,
@@ -147,7 +153,7 @@
                     device_id_type=MESH,
                 )
 
-        @pl.when(there[side] > my_far)
+        @pl.when(reached[side] & (there[side] > my_far))
         def _():
             pl.semaphore_signal(
                 barrier,
@@ -156,15 +162,13 @@
                 device_id_type=MESH,
             )
 
-    for copy in small:
-        copy.start()
-    own_in.start()
     heard = my_rank
     for side in range(2):
-        heard = heard + jnp.where(near_rank(beside[side]) < my_near_rank, 1, 0)
+        lower = near_rank(beside[side]) < my_near_rank
+        heard = heard + jnp.where((chip == 0) & lower, 1, 0)
         earlier = there[side] < my_far
-        heard = heard + jnp.where(earlier, 1, 0)
-        heard = heard + jnp.where(earlier & (chip == ends[side]), chips, 0)
+        heard = heard + jnp.where(earlier & reached[side], 1, 0)
+        heard = heard + jnp.where(earlier & (chip == ends[side]), reach[side], 0)
 
     @pl.when(heard > 0)
     def _():
@@ -208,11 +212,18 @@
     for j in range(1, group):
         @pl.when(rank(peer_of(j)) < my_rank)
         def _():
-            exchange(0, peer_of(j)).start()
             pl.semaphore_signal(
                 hello.at[me], inc=1, device_id=at_frame(peer_of(j)), device_id_type=MESH
             )
 
+    for j in range(1, group):
+        @pl.when(rank(peer_of(j)) < my_rank)
+        def _():
+            exchange(0, peer_of(j)).start()
+
+    for copy in small:
+        copy.start()
+    own_in.start()
     for peer in (*range(1, group), 0):
         @pl.when(rank(peer) > my_rank)
         def _():
@@ -226,7 +237,7 @@
         keep(chunk).start()
 
     for side in range(2):
-        @pl.when(near_rank(beside[side]) < my_near_rank)
+        @pl.when((chip == 0) & (near_rank(beside[side]) < my_near_rank))
         def _():
             pl.semaphore_signal(
                 near_hello.at[1 - side],
@@ -236,7 +247,7 @@
             )
 
     for side in range(2):
-        @pl.when(there[side] < my_far)
+        @pl.when(reached[side] & (there[side] < my_far))
         def _():
             pl.semaphore_signal(
                 far_hello,
@@ -248,21 +259,30 @@
     for copy in small:
         copy.wait()
 
-    def far_copy(side, z):
+    def far_copy(side, source):
         return pltpu.make_async_remote_copy(
             src_ref=codes.at[0],
-            dst_ref=far_codes.at[my_far],
-            send_sem=far_send.at[side, z],
+            dst_ref=far_codes.at[source],
+            send_sem=far_send.at[side],
             recv_sem=far_recv.at[side],
-            device_id=at_far(there[side], z),
+            device_id=at_far(there[side], 0),
             device_id_type=MESH,
         )
 
     def far_start(side, when):
         @pl.when((chip == ends[side]) & when)
         def _():
-            for z in range(chips):
-                far_copy(side, z).start()
+            far_copy(side, my_far).start()
+
+    def row_copy(z):
+        return pltpu.make_async_remote_copy(
+            src_ref=row_out,
+            dst_ref=row_in,
+            send_sem=row_send.at[z],
+            recv_sem=row_recv,
+            device_id=at_far(there[1], z),
+            device_id_type=MESH,
+        )
 
     for side in range(2):
         far_start(side, there[side] < my_far)
@@ -307,19 +327,10 @@
     for side in range(2):
         @pl.when((chip == ends[side]) & (there[side] > my_far))
         def _():
-            pl.semaphore_wait(far_hello, chips)
+            pl.semaphore_wait(far_hello, reach[side])
 
         far_start(side, there[side] > my_far)
     own_code.wait()
-    for side in range(2):
-        pltpu.make_async_remote_copy(
-            src_ref=codes.at[0],
-            dst_ref=far_codes.at[there[1 - side]],
-            send_sem=far_send.at[side, 0],
-            recv_sem=far_recv.at[side],
-            device_id=at_far(there[side], 0),
-            device_id_type=MESH,
-        ).wait_recv()
 
     hops = (near // 2, (near - 1) // 2)
 
@@ -345,27 +356,43 @@
             device_id_type=MESH,
         )
 
-    for side in range(2):
-        @pl.when(near_rank(beside[side]) > my_near_rank)
-        def _():
-            pl.semaphore_wait(near_hello.at[side], 1)
-
-        near_copy(side, 0).start()
-    near_own = pltpu.make_async_copy(far_codes, all_codes.at[my_near], code_sem.at[1])
-    near_own.start()
-    for hop in range(hops[0]):
+    def row_of(wanted):
+        row = jnp.zeros(codes.shape[1:], jnp.float32)
+        for i in range(clips):
+            row = row + jnp.where(
+                clip_ids[i] == wanted, all_codes[i % near, i // near], 0.0
+            )
+        return row
+
+    @pl.when(chip == 0)
+    def _():
         for side in range(2):
-            if hop < hops[side]:
-                near_arrived(side, hop).wait_recv()
-            if hop + 1 < hops[side]:
-                near_copy(side, hop + 1).start()
-    near_own.wait()
-
-    by_clip = jnp.zeros(codes.shape[1:], jnp.float32)
-    for i in range(clips):
-        by_clip = by_clip + jnp.where(
-            clip_ids[i] == clip, all_codes[i % near, i // near], 0.0
-        )
+            far_copy(side, there[1 - side]).wait_recv()
+        for side in range(2):
+            @pl.when(near_rank(beside[side]) > my_near_rank)
+            def _():
+                pl.semaphore_wait(near_hello.at[side], 1)
+
+            near_copy(side, 0).start()
+        near_own = pltpu.make_async_copy(
+            far_codes, all_codes.at[my_near], code_sem.at[1]
+        )
+        near_own.start()
+        for hop in range(hops[0]):
+            for side in range(2):
+                if hop < hops[side]:
+                    near_arrived(side, hop).wait_recv()
+                if hop + 1 < hops[side]:
+                    near_copy(side, hop + 1).start()
+        near_own.wait()
+        row_out[...] = row_of(there[1] * near + my_near)
+        row_in[...] = row_of(clip)
+
+    @pl.when(chip > 0)
+    def _():
+        row_copy(1).wait_recv()
+
+    by_clip = row_in[...]
     slot_of = lax.broadcasted_iota(jnp.int32, (slots, 1), 0)
     time_of = jnp.zeros((slots, 1), jnp.int32)
     for s in range(slots):
@@ -380,6 +407,11 @@
         preferred_element_type=jnp.float32,
     )
 
+    @pl.when(chip == 0)
+    def _():
+        for z in range(1, chips):
+            row_copy(z).start()
+
     def give(chunk, j):
         peer = peer_of(j)
         return pltpu.make_async_remote_copy(
@@ -440,11 +472,15 @@
     for side in range(2):
         @pl.when(chip == ends[side])
         def _():
-            for z in range(chips):
-                far_copy(side, z).wait_send()
-    for side in range(2):
-        for hop in range(hops[side]):
-            near_copy(side, hop).wait_send()
+            far_copy(side, my_far).wait_send()
+
+    @pl.when(chip == 0)
+    def _():
+        for side in range(2):
+            for hop in range(hops[side]):
+                near_copy(side, hop).wait_send()
+        for z in range(1, chips):
+            row_copy(z).wait_send()
 
 
 def move(source, out, sems):
@@ -491,6 +527,8 @@
                 pltpu.VMEM(weight.shape, f32),
                 pltpu.VMEM((FAR, *codes.shape[1:]), f32),
                 pltpu.VMEM((near, FAR, *codes.shape[1:]), f32),
+                pltpu.VMEM(codes.shape[1:], f32),
+                pltpu.VMEM(codes.shape[1:], f32),
                 pltpu.VMEM((slots, width), f32),
                 pltpu.VMEM((rows, rows), f32),
                 pltpu.VMEM((3, frames, patches, width), bf16),
@@ -498,8 +536,10 @@
                 pltpu.VMEM((group, frames, share, width), bf16),
                 pltpu.VMEM((group, frames, share, width), bf16),
                 dma((5,)),
-                dma((2, group // CORES)),
                 dma((2,)),
+                dma((2,)),
+                dma((group // CORES,)),
+                dma(()),
                 pltpu.SemaphoreType.REGULAR,
                 pltpu.SemaphoreType.REGULAR((group,)),
                 pltpu.SemaphoreType.REGULAR((2,)),

time: 66.1 us -> 66 us (level)
  no operation moved by 1% of the time
where the time goes in v5:
time: 66 us; the launch traced here: 65.9 us
  Pallas kernels  65.9 us (100%)
    pallas_call x1, Pallas kernels, local(): pl.pallas_call(functools.partial(kernel, (clips, group, frames, patches,...  65 us

profile of v5, /device:TPU:1, one launch (start us, length us, event | category | flops | bytes accessed | tf_op | source)
XLA Modules:
  0.0 65.9 jit_solution(10378896639708212898)
XLA Ops:
  0.0 65.0 %shard_map.64.source = bf16[1,2,128,1280]{3,2,1,0:T(8,128)(2,1)S(1)} custom-call(s32[24]{0:T(128)} %clip_ids_in.1, s32[16]{0:T(128)} %frame_map_in.1, s32[1,16]{1,0:T(1,128)} %segments_in.1, f32[1,16,32]{2,1,0:T(8,128)} %codes_in.1, f32[32,1280]{1,0:T(8,128)} %weight_in.1, bf16[6,1,2,128,1280]{4,3,2,1,0:T(8,128)(2,1)} %projected.1), custom_call_target="tpu_custom_call" | custom-call | tf_op jit(solution)/shard_map/pallas_call | solution.py:517
  65.0 0.9 %shard_map.65 = bf16[1,2,128,1280]{3,2,1,0:T(8,128)(2,1)} custom-call(bf16[1,2,128,1280]{3,2,1,0:T(8,128)(2,1)S(1)} %shard_map.64.source), custom_call_target="tpu_custom_call" | custom-call | tf_op jit(solution)/shard_map/pallas_call | solution.py:566

commit v6 on v5

--- a/solution.py
+++ b/solution.py
@@ -11,7 +11,7 @@
 E = 128
 FAR = 3
 CORES = 2
-SIZES = (5, 3, 2)
+SIZES = (4, 4, 2)
 MOVES = 4
 
 
@@ -423,6 +423,9 @@
             device_id_type=MESH,
         )
 
+    def held(j):
+        return (chip == chips // 2) & (peer_of(j) // CORES == chips // 2 - 1)
+
     def give_self(chunk):
         return pltpu.make_async_copy(
             done.at[me, :, :, lanes_of(chunk)],
@@ -450,8 +453,19 @@
         keep(chunk).wait()
         lax.fori_loop(starts[chunk], starts[chunk] + SIZES[chunk], attend, 0)
         for j in range(1, group):
-            give(chunk, j).start()
+            if chunk == chunks - 2:
+                @pl.when(jnp.logical_not(held(j)))
+                def _():
+                    give(chunk, j).start()
+            else:
+                give(chunk, j).start()
         give_self(chunk).start()
+        if chunk == chunks - 1:
+            for j in range(1, group):
+                @pl.when(held(j))
+                def _():
+                    give(chunk - 1, j).start()
+
 
     for chunk in range(chunks):
         for j in range(1, group):

time: 66 us -> 64.5 us (0.977)
  Pallas kernels: 65.9 us -> 64.4 us
    pallas_call x1, Pallas kernels: 65 us -> 63.5 us  [local(): pl.pallas_call(functools.partial(kernel, (clips, group, frames, patches,...]
where the time goes in v6:
time: 64.5 us; the launch traced here: 64.4 us
  Pallas kernels  64.4 us (100%)
    pallas_call x1, Pallas kernels, local(): pl.pallas_call(functools.partial(kernel, (clips, group, frames, patches,...  63.5 us

profile of v6, /device:TPU:1, one launch (start us, length us, event | category | flops | bytes accessed | tf_op | source)
XLA Modules:
  0.0 64.4 jit_solution(2733035060811529456)
XLA Ops:
  0.0 63.5 %shard_map.64.source = bf16[1,2,128,1280]{3,2,1,0:T(8,128)(2,1)S(1)} custom-call(s32[24]{0:T(128)} %clip_ids_in.1, s32[16]{0:T(128)} %frame_map_in.1, s32[1,16]{1,0:T(1,128)} %segments_in.1, f32[1,16,32]{2,1,0:T(8,128)} %codes_in.1, f32[32,1280]{1,0:T(8,128)} %weight_in.1, bf16[6,1,2,128,1280]{4,3,2,1,0:T(8,128)(2,1)} %projected.1), custom_call_target="tpu_custom_call" | custom-call | tf_op jit(solution)/shard_map/pallas_call | solution.py:531
  63.5 0.9 %shard_map.65 = bf16[1,2,128,1280]{3,2,1,0:T(8,128)(2,1)} custom-call(bf16[1,2,128,1280]{3,2,1,0:T(8,128)(2,1)S(1)} %shard_map.64.source), custom_call_target="tpu_custom_call" | custom-call | tf_op jit(solution)/shard_map/pallas_call | solution.py:580

commit v7 on v6

--- a/solution.py
+++ b/solution.py
@@ -11,7 +11,7 @@
 E = 128
 FAR = 3
 CORES = 2
-SIZES = (4, 4, 2)
+SIZES = (3, 4, 3)
 MOVES = 4
 
 

time: 64.5 us -> 64.6 us (level)
  no operation moved by 1% of the time
where the time goes in v7:
time: 64.6 us; the launch traced here: 64.4 us
  Pallas kernels  64.4 us (100%)
    pallas_call x1, Pallas kernels, local(): pl.pallas_call(functools.partial(kernel, (clips, group, frames, patches,...  63.5 us

profile of v7, /device:TPU:1, one launch (start us, length us, event | category | flops | bytes accessed | tf_op | source)
XLA Modules:
  0.0 64.4 jit_solution(12137722226595399219)
XLA Ops:
  0.0 63.5 %shard_map.64.source = bf16[1,2,128,1280]{3,2,1,0:T(8,128)(2,1)S(1)} custom-call(s32[24]{0:T(128)} %clip_ids_in.1, s32[16]{0:T(128)} %frame_map_in.1, s32[1,16]{1,0:T(1,128)} %segments_in.1, f32[1,16,32]{2,1,0:T(8,128)} %codes_in.1, f32[32,1280]{1,0:T(8,128)} %weight_in.1, bf16[6,1,2,128,1280]{4,3,2,1,0:T(8,128)(2,1)} %projected.1), custom_call_target="tpu_custom_call" | custom-call | tf_op jit(solution)/shard_map/pallas_call | solution.py:531
  63.5 0.9 %shard_map.65 = bf16[1,2,128,1280]{3,2,1,0:T(8,128)(2,1)} custom-call(bf16[1,2,128,1280]{3,2,1,0:T(8,128)(2,1)S(1)} %shard_map.64.source), custom_call_target="tpu_custom_call" | custom-call | tf_op jit(solution)/shard_map/pallas_call | solution.py:580

commit v8 on v6

--- a/solution.py
+++ b/solution.py
@@ -424,7 +424,7 @@
         )
 
     def held(j):
-        return (chip == chips // 2) & (peer_of(j) // CORES == chips // 2 - 1)
+        return (chip >= chips // 2) & (peer_of(j) // CORES == chips // 2 - 1)
 
     def give_self(chunk):
         return pltpu.make_async_copy(

time: 64.5 us -> 64.7 us (level)
  no operation moved by 1% of the time
where the time goes in v8:
time: 64.7 us; the launch traced here: 64.6 us
  Pallas kernels  64.6 us (100%)
    pallas_call x1, Pallas kernels, local(): pl.pallas_call(functools.partial(kernel, (clips, group, frames, patches,...  63.7 us

profile of v8, /device:TPU:1, one launch (start us, length us, event | category | flops | bytes accessed | tf_op | source)
XLA Modules:
  0.0 64.6 jit_solution(3619087177026414825)
XLA Ops:
  0.0 63.7 %shard_map.64.source = bf16[1,2,128,1280]{3,2,1,0:T(8,128)(2,1)S(1)} custom-call(s32[24]{0:T(128)} %clip_ids_in.1, s32[16]{0:T(128)} %frame_map_in.1, s32[1,16]{1,0:T(1,128)} %segments_in.1, f32[1,16,32]{2,1,0:T(8,128)} %codes_in.1, f32[32,1280]{1,0:T(8,128)} %weight_in.1, bf16[6,1,2,128,1280]{4,3,2,1,0:T(8,128)(2,1)} %projected.1), custom_call_target="tpu_custom_call" | custom-call | tf_op jit(solution)/shard_map/pallas_call | solution.py:531
  63.7 0.9 %shard_map.65 = bf16[1,2,128,1280]{3,2,1,0:T(8,128)(2,1)} custom-call(bf16[1,2,128,1280]{3,2,1,0:T(8,128)(2,1)S(1)} %shard_map.64.source), custom_call_target="tpu_custom_call" | custom-call | tf_op jit(solution)/shard_map/pallas_call | solution.py:580
